TPU v7x, 256 devices: a whole 4x4x8 slice. The times are simulated.
256 devices in a mesh: dp: 8 (over y, core), expert: 32 (over z, x).
Axes of the slice: x: 4, y: 4, z: 8, core: 2. Of those that a mesh axis runs over, the one named last changes fastest.
Arguments:
- route_experts: int32 [32768, 8], P(('dp', 'expert')), may hold values from 0 to 255, all different within a row; in each aligned block of 128 rows (0 to 127, 128 to 255, ...) at most 5 rows name the same one
- router_gate_weight: float32 [32768, 8], P(('dp', 'expert')), may hold values from 0.02 to 0.3
- forget_mask: int32 [32768], P(('dp', 'expert')), may hold values 0 or 1
- retain_mask: int32 [32768], P(('dp', 'expert')), may hold values 0 or 1
- layer_output: bfloat16 [32768, 3584], P(('dp', 'expert')), may hold values from -6 to 6
- frozen_output: bfloat16 [32768, 3584], P(('dp', 'expert')), may hold values from -6 to 6
- control_vector: float32 [3584], replicated, may hold values from 0.1 to 1
- saved_hidden: bfloat16 [2048, 160, 2048], P(('dp', 'expert')), may hold values from -6 to 6
- adapter_in: bfloat16 [2048, 16384], P('dp', 'expert'), may hold values from -0.125 to 0.125
- adapter_out: bfloat16 [3584, 16384], P('dp', 'expert'), may hold values from -0.09375 to 0.09375
Outputs:
- grad_in: float32 [2048, 16384], P('dp', 'expert')
- grad_out: float32 [3584, 16384], P('dp', 'expert')
Inputs may be any that keep to these rules, and one draw needn't show every extreme that they name: `route_experts`: each row names 8 different experts; within the 128 rows of one device no expert is named more than 5 times, a bound that some block reaches.
All inputs are finite; a program needn't handle non-finite values. No bound on the sum of `forget_mask` or of `retain_mask` on one device may be relied on, other than what follows from the above.
Results may differ from a plain program's by a relative error of at most 0.0041.
Values may be sent and summed in bfloat16 or wider, within the bound.
No kernel may reach another device: no remote copies, remote signals or barrier semaphores. Data moves between devices by JAX's collectives and lax.ppermute only.
A program may use at most 128 MiB of HBM per device.

v0:
```python
import jax
import jax.numpy as jnp
from jax import lax
from jax.sharding import PartitionSpec as P

steer_coef = 20.0
retain_weight = 1.5
adapter_scale_factor = 2.0
grad_coef = 0.0625


def route_slots(experts_flat, count_all, capacity):
    onehot = (experts_flat[:, None] == jnp.arange(count_all, dtype=jnp.int32)[None, :]).astype(
        jnp.int32
    )
    running = jnp.cumsum(onehot, axis=0) - 1
    within = jnp.sum(onehot * running, axis=1)
    return experts_flat * capacity + within


def token_cotangent(layer_output, frozen_output, forget_mask, retain_mask, control_vector):
    unit = control_vector / jnp.sqrt(jnp.sum(control_vector * control_vector))
    current = layer_output.astype(jnp.float32)
    forget_term = current - steer_coef * unit[None, :]
    retain_term = current - frozen_output.astype(jnp.float32)
    forget_weight = forget_mask.astype(jnp.float32)[:, None]
    retain_part = retain_mask.astype(jnp.float32)[:, None]
    return grad_coef * (forget_weight * forget_term + retain_weight * retain_part * retain_term)


def local(
    route_experts,
    router_gate_weight,
    forget_mask,
    retain_mask,
    layer_output,
    frozen_output,
    control_vector,
    saved_hidden,
    adapter_in,
    adapter_out,
):
    experts_here = saved_hidden.shape[0]
    slot_count = saved_hidden.shape[1]
    hidden_width = saved_hidden.shape[2]
    feature_width = layer_output.shape[1]
    rank_width = adapter_in.shape[1] // experts_here
    expert_devices = lax.axis_size("expert")
    data_devices = lax.axis_size("dp")
    capacity = slot_count // expert_devices
    experts_all = experts_here * expert_devices
    output_gradient = token_cotangent(
        layer_output, frozen_output, forget_mask, retain_mask, control_vector
    )
    value_rows = (
        (router_gate_weight[:, :, None] * adapter_scale_factor * output_gradient[:, None, :])
        .reshape(-1, feature_width)
        .astype(jnp.bfloat16)
    )
    expert_slot_index = route_slots(route_experts.reshape(-1), experts_all, capacity)
    outgoing = (
        jnp.zeros((experts_all * capacity, feature_width), jnp.bfloat16)
        .at[expert_slot_index]
        .set(value_rows)
    )
    outgoing = outgoing.reshape(experts_all, capacity, feature_width)
    segment = lax.all_gather(adapter_in, "dp", axis=0, tiled=True)
    rows_now = segment.shape[0]
    hidden_part = saved_hidden
    factor = segment.reshape(rows_now, experts_here, rank_width)
    codes = jnp.einsum(
        "esf,fer->esr", hidden_part, factor, preferred_element_type=jnp.float32
    ).astype(jnp.bfloat16)
    arrived = lax.all_to_all(outgoing, "expert", split_axis=0, concat_axis=1, tiled=True)
    segment = lax.all_gather(adapter_out, "dp", axis=0, tiled=True)
    rows_now = segment.shape[0]
    arrived_part = arrived
    factor = segment.reshape(rows_now, experts_here, rank_width)
    back = jnp.einsum(
        "esd,der->esr", arrived_part, factor, preferred_element_type=jnp.float32
    ).astype(jnp.bfloat16)
    arrived_part = arrived
    product = jnp.einsum("esd,esr->der", arrived_part, codes, preferred_element_type=jnp.float32)
    grad_out = lax.psum_scatter(
        product.reshape(
            feature_width // data_devices * lax.axis_size("dp"), experts_here * rank_width
        ),
        "dp",
        scatter_dimension=0,
        tiled=True,
    )
    hidden_part = saved_hidden
    product = jnp.einsum("esf,esr->fer", hidden_part, back, preferred_element_type=jnp.float32)
    grad_in = lax.psum_scatter(
        product.reshape(
            hidden_width // data_devices * lax.axis_size("dp"), experts_here * rank_width
        ),
        "dp",
        scatter_dimension=0,
        tiled=True,
    )
    return (grad_in, grad_out)


def solution(mesh):
    return jax.shard_map(
        local,
        mesh=mesh,
        in_specs=(
            P(("dp", "expert"), None),
            P(("dp", "expert"), None),
            P(("dp", "expert")),
            P(("dp", "expert")),
            P(("dp", "expert"), None),
            P(("dp", "expert"), None),
            P(),
            P(("dp", "expert"), None, None),
            P("dp", "expert"),
            P("dp", "expert"),
        ),
        out_specs=(P("dp", "expert"), P("dp", "expert")),
        check_vma=False,
    )
```

profile of v0, /device:TPU:1, one launch (start us, length us, event | category | flops | bytes accessed | tf_op | source)
XLA Modules:
  0.0 537.4 jit_solution(12084886963748283533)
XLA Ops:
  7.2 0.0 copy-start.2
  7.2 0.0 copy-start.4
  7.2 0.0 copy-start.5
  7.2 0.0 copy-start.3
  7.2 0.0 copy-start
  7.2 0.9 copy.28
  8.1 0.1 eq.29
  8.2 0.1 eq.25
  8.3 0.7 broadcast_multiply_fusion.1
  9.0 0.1 copy.30
  9.1 0.2 fusion.21
  9.3 0.1 add_add_fusion
  9.4 0.3 copy.31
  9.7 0.1 copy.27
  9.8 0.1 mul.85
  9.9 0.0 copy-done.2
  10.0 0.6 multiply_reduce_fusion
  11.3 0.0 copy-done.4
  11.3 0.0 copy-done.5
  11.3 0.0 copy-done.3
  11.3 0.1 copy.32
  11.4 0.1 mul.89
  11.5 0.4 fusion.20
  11.9 0.0 copy-done
  11.9 1.7 fusion.12
  13.6 15.6 %scatter_custom_fusion = bf16[1280,3584]{1,0:T(8,128)(2,1)} fusion(s32[1024]{0:T(1024)S(1)} %bitcast.38, f32[128,3584]{1,0:T(8,128)S(1)} %fusion.12, f32[1024]{0:T(1024)S(1)} %mul.89, bf16[]{:T(256)} %constant.10.clone.1), kind=kCustom, calls=%fused_computation.7 | custom fusion | flops 7340032 | bytes 11014146 | tf_op jit(solution)/shard_map/scatter | solution.py:64
  29.2 14.6 %reshape.80 = bf16[256,5,3584]{2,1,0:T(8,128)(2,1)} reshape(bf16[1280,3584]{1,0:T(8,128)(2,1)} %scatter_custom_fusion) | data formatting | bytes 18350080 | tf_op jit(solution)/shard_map/reshape | solution.py:66
  43.8 0.0 copy-start.1
  43.8 12.1 %all-to-all-start = ((bf16[256,5,3584]{2,1,0:T(8,128)(2,1)}), bf16[256,5,3584]{2,1,0:T(8,128)(2,1)}, u32[]{:S(2)}, u32[]{:S(2)}) async-start(bf16[256,5,3584]{2,1,0:T(8,128)(2,1)} %reshape.80), calls=%async_computation | async-start | bytes 29360128 | tf_op jit(solution)/shard_map/all_to_all | solution.py:74
  55.9 0.0 all-gather.3.cloned.1.call-start
  56.0 0.7 all-gather.3.cloned.1.call-update
  56.6 0.0 all-gather.5.cloned.1.call-start
  56.7 0.0 copy-done.1
  56.7 0.8 copy.38
  57.5 0.0 all-gather.5.cloned.1.call-update
  57.6 0.0 reduce-scatter.3.cloned.1.call-start
  57.6 35.5 %all-gather.3.cloned.1.call-done = bf16[3584,512]{1,0:T(8,128)(2,1)} async-done(((bf16[448,512]{1,0:T(8,128)(2,1)}), bf16[3584,512]{1,0:T(8,128)(2,1)}) %all-gather.3.cloned.1.call-update) | async-done | bytes 3670032 | tf_op jit(solution)/shard_map/all_gather | solution.py:75
  93.1 5.9 %copy.35 = bf16[3584,512]{0,1:T(8,128)(2,1)} copy(bf16[3584,512]{1,0:T(8,128)(2,1)} %all-gather.3.cloned.1.call-done) | data formatting | bytes 7340032 | tf_op jit(solution)/shard_map/all_gather | solution.py:75
  99.0 296.3 %all-to-all-done = bf16[256,5,3584]{2,1,0:T(8,128)(2,1)} async-done(((bf16[256,5,3584]{2,1,0:T(8,128)(2,1)}), bf16[256,5,3584]{2,1,0:T(8,128)(2,1)}, u32[]{:S(2)}, u32[]{:S(2)}) %all-to-all-start) | async-done | bytes 9175072 | tf_op jit(solution)/shard_map/all_to_all | solution.py:74
  395.3 11.4 %copy.34 = bf16[8,32,5,3584]{3,0,2,1:T(8,128)(2,1)} copy(bf16[8,32,5,3584]{3,2,0,1:T(8,128)(2,1)} %bitcast.8) | data formatting | bytes 18350080 | tf_op jit(solution)/shard_map/all_to_all | solution.py:74
  406.7 12.2 %fusion.18 = f32[8,64,2048]{2,1,0:T(8,128)} fusion(bf16[8,160,2048]{2,1,0:T(8,128)(2,1)} %param.17, bf16[3584,8,64]{0,2,1:T(8,128)(2,1)} %bitcast.35, bf16[8,160,3584]{2,0,1:T(8,128)(2,1)} %bitcast.31), kind=kOutput, calls=%fused_computation.19 | convolution fusion | flops 922828800 | bytes 22282240 | tf_op jit(solution)/shard_map/esf,esr->fer/dot_general | solution.py:93
  418.8 5.3 copy.37
  424.2 0.0 reduce-scatter.3.cloned.1.call-update
  424.2 0.3 reduce-scatter.5.cloned.1.call-start
  424.5 0.0 all-gather.5.cloned.1.call-done
  424.5 16.2 %fusion.1 = f32[8,64,3584]{2,1,0:T(8,128)} fusion(bf16[8,160,3584]{2,0,1:T(8,128)(2,1)} %bitcast.32, bf16[8,160,2048]{2,1,0:T(8,128)(2,1)} %param.17, bf16[2048,8,64]{0,2,1:T(8,128)(2,1)} %bitcast.36), kind=kOutput, calls=%fused_computation.3 | convolution fusion | flops 922828800 | bytes 23855104 | tf_op jit(solution)/shard_map/esd,esr->der/dot_general | solution.py:83
  440.8 8.4 %copy.40 = f32[3584,512]{1,0:T(8,128)} copy(f32[3584,512]{0,1:T(8,128)} %bitcast.33) | data formatting | bytes 14680064 | tf_op jit(solution)/shard_map/reshape | solution.py:85
  449.1 0.0 reduce-scatter.5.cloned.1.call-update
  449.1 27.5 %reduce-scatter.3.cloned.1.call-done = f32[256,512]{1,0:T(8,128)} async-done(((f32[2048,512]{1,0:T(8,128)}), f32[256,512]{1,0:T(8,128)}) %reduce-scatter.3.cloned.1.call-update) | async-done | bytes 524304 | tf_op jit(solution)/shard_map/reduce_scatter | solution.py:94
  476.6 54.2 %reduce-scatter.5.cloned.1.call-done = f32[448,512]{1,0:T(8,128)} async-done(((f32[3584,512]{1,0:T(8,128)}), f32[448,512]{1,0:T(8,128)}) %reduce-scatter.5.cloned.1.call-update) | async-done | bytes 917520 | tf_op jit(solution)/shard_map/reduce_scatter | solution.py:84
  (8 shorter events, 0.1 us)
Async XLA Ops:
  7.2 2.8 copy-start.2
  7.2 4.1 copy-start.4
  7.2 4.1 copy-start.5
  7.2 4.1 copy-start.3
  7.2 4.7 copy-start
  43.8 12.9 %copy-start.1 = (bf16[256,512]{1,0:T(8,128)(2,1)S(1)}, bf16[256,512]{1,0:T(8,128)(2,1)}, u32[]{:S(2)}) copy-start(bf16[256,512]{1,0:T(8,128)(2,1)} %param.18) | copy-start | bytes 786436
  43.8 351.5 %all-to-all-start = ((bf16[256,5,3584]{2,1,0:T(8,128)(2,1)}), bf16[256,5,3584]{2,1,0:T(8,128)(2,1)}, u32[]{:S(2)}, u32[]{:S(2)}) async-start(bf16[256,5,3584]{2,1,0:T(8,128)(2,1)} %reshape.80), calls=%async_computation | async-start | bytes 29360128 | tf_op jit(solution)/shard_map/all_to_all | solution.py:74
  55.9 37.2 %all-gather.3.cloned.1.call-start = ((), (), s32[]{:S(2)}) async-start(), calls=%async_computation.3 | async-start | bytes 4128768 | tf_op jit(solution)/shard_map/all_gather | solution.py:75
  56.6 367.9 %all-gather.5.cloned.1.call-start = ((), (), s32[]{:S(2)}) async-start(), calls=%async_computation.5 | async-start | bytes 2359296 | tf_op jit(solution)/shard_map/all_gather | solution.py:67
  57.6 419.0 %reduce-scatter.3.cloned.1.call-start = ((), (), s32[]{:S(2)}) async-start(), calls=%async_computation.4 | async-start | bytes 4718592 | tf_op jit(solution)/shard_map/reduce_scatter | solution.py:94
  424.2 106.6 %reduce-scatter.5.cloned.1.call-start = ((), (), s32[]{:S(2)}) async-start(), calls=%async_computation.6 | async-start | bytes 8257536 | tf_op jit(solution)/shard_map/reduce_scatter | solution.py:84
Sparse Core Ops, SparseCore 0:
  58.6 34.4 all-gather.2
  95.5 29.2 all-gather.4
  424.3 52.2 reduce-scatter.2
  479.6 51.1 reduce-scatter.4
where the time goes:
time: 538 us; the launch traced here: 537 us
  waiting for transfers between devices  414 us (77%)
  local copies, waits for them, and re-layouts  48.3 us (9%)
  matrix products  28.4 us (5%)
  other arithmetic  19.3 us (4%)
  between operations  14.6 us (3%)
  starting transfers between devices  12.5 us (2%)
    all_to_all x1, waiting for transfers between devices, local(): lax.all_to_all(outgoing, 'expert', split_axis=0, concat_axis=1, tiled=True)  296 us
    reduce_scatter x1, waiting for transfers between devices, local(): lax.psum_scatter(product.reshape(feature_width // data_devices * lax.axis...  54.2 us
    all_gather x1, waiting for transfers between devices, local(): segment = lax.all_gather(adapter_out, 'dp', axis=0, tiled=True)  35.5 us
    reduce_scatter x1, waiting for transfers between devices, local(): lax.psum_scatter(product.reshape(hidden_width // data_devices * lax.axis_...  27.5 us
    dot_general x1, matrix products, local(): jnp.einsum('esd,esr->der', arrived_part, codes, preferred_element_type=jn...  16.2 us
    scatter x1, other arithmetic, local(): outgoing = jnp.zeros((experts_all * capacity, feature_width), jnp.bfloat1...  15.6 us
    reshape x1, local copies, waits for them, and re-layouts, local(): outgoing = outgoing.reshape(experts_all, capacity, feature_width)  14.6 us
    dot_general x1, matrix products, local(): jnp.einsum('esf,esr->fer', hidden_part, back, preferred_element_type=jnp....  12.2 us
  transfers between devices with their start and end apart: 5, of which 4 were waited for; matrix products, arithmetic and copies ran while one was open for 11% of the time, Pallas kernels for 0%

commit v1 on v0

--- a/solution.py
+++ b/solution.py
@@ -71,7 +71,12 @@
     codes = jnp.einsum(
         "esf,fer->esr", hidden_part, factor, preferred_element_type=jnp.float32
     ).astype(jnp.bfloat16)
-    arrived = lax.all_to_all(outgoing, "expert", split_axis=0, concat_axis=1, tiled=True)
+    arrived = jnp.concatenate(
+        lax.all_to_all(
+            jnp.stack(jnp.split(outgoing, lax.axis_size("expert"), axis=0)), "expert", 0, 0
+        ),
+        axis=1,
+    )
     segment = lax.all_gather(adapter_out, "dp", axis=0, tiled=True)
     rows_now = segment.shape[0]
     arrived_part = arrived

time: 538 us -> 483 us (0.90)
  waiting for transfers between devices: 414 us -> 277 us
  local copies, waits for them, and re-layouts: 48.3 us -> 126 us
    all_to_all x1, waiting for transfers between devices: 296 us -> 162 us  [local(): lax.all_to_all(jnp.stack(jnp.split(outgoing, lax.axis_size('expert'), axi...]
    another operation x2 -> x36, local copies, waits for them, and re-layouts: 0.01 us -> 53.8 us  [the longest x34 53.8 us: local(): jnp.stack(jnp.split(outgoing, lax.axis_size('expert'), axis=0))]
    unnamed x14 -> x55, local copies, waits for them, and re-layouts: 1.74 us -> 43.3 us
    reshape x1 -> x0, local copies, waits for them, and re-layouts: 14.6 us -> none  [local(): outgoing = outgoing.reshape(experts_all, capacity, feature_width)]
    all_to_all x1 -> x0, local copies, waits for them, and re-layouts: 11.4 us -> none  [local(): lax.all_to_all(outgoing, 'expert', split_axis=0, concat_axis=1, tiled=True)]
    split x0 -> x2, local copies, waits for them, and re-layouts: none -> 8.02 us  [local(): jnp.split(outgoing, lax.axis_size('expert'), axis=0)]
  transfers between devices with their start and end apart: 5 -> 5, of which waited for: 4 -> 4; matrix products, arithmetic and copies ran while one was open for 11% -> 10% of each run, Pallas kernels for 0% -> 0%
where the time goes in v1:
time: 483 us; the launch traced here: 481 us
  waiting for transfers between devices  277 us (57%)
  local copies, waits for them, and re-layouts  126 us (26%)
  matrix products  28.5 us (6%)
  other arithmetic  23 us (5%)
  between operations  14.7 us (3%)
  starting transfers between devices  12.5 us (3%)
    all_to_all x1, waiting for transfers between devices, local(): lax.all_to_all(jnp.stack(jnp.split(outgoing, lax.axis_size('expert'), axi...  162 us
    reduce_scatter x1, waiting for transfers between devices, local(): lax.psum_scatter(product.reshape(feature_width // data_devices * lax.axis...  54.2 us
    another operation x34, local copies, waits for them, and re-layouts, local(): jnp.stack(jnp.split(outgoing, lax.axis_size('expert'), axis=0))  53.8 us
    unnamed x55, local copies, waits for them, and re-layouts  43.3 us
    all_gather x1, waiting for transfers between devices, local(): segment = lax.all_gather(adapter_out, 'dp', axis=0, tiled=True)  35.2 us
    reduce_scatter x1, waiting for transfers between devices, local(): lax.psum_scatter(product.reshape(hidden_width // data_devices * lax.axis_...  24.3 us
    dot_general x1, matrix products, local(): jnp.einsum('esd,esr->der', arrived_part, codes, preferred_element_type=jn...  16.2 us
    scatter x1, other arithmetic, local(): outgoing = jnp.zeros((experts_all * capacity, feature_width), jnp.bfloat1...  15.7 us
  transfers between devices with their start and end apart: 5, of which 4 were waited for; matrix products, arithmetic and copies ran while one was open for 10% of the time, Pallas kernels for 0%

profile of v1, /device:TPU:1, one launch (start us, length us, event | category | flops | bytes accessed | tf_op | source)
XLA Modules:
  0.0 481.2 jit_solution(2297948641117503773)
XLA Ops:
  9.8 1.3 multiply_reduce_fusion
  15.1 2.0 fusion.12
  17.1 15.7 %scatter_custom_fusion = bf16[1280,3584]{1,0:T(8,128)(2,1)} fusion(s32[1024]{0:T(1024)S(1)} %bitcast.35, f32[128,3584]{1,0:T(8,128)S(1)} %fusion.12, f32[1024]{0:T(1024)S(1)} %mul.89, bf16[]{:T(256)} %constant.10.clone.1), kind=kCustom, calls=%fused_computation.7 | custom fusion | flops 7340032 | bytes 11014146 | tf_op jit(solution)/shard_map/scatter | solution.py:64
  32.8 3.1 fusion.25
  35.9 4.9 %fusion.24 = (bf16[40,3584]{1,0:T(8,128)(2,1)}, bf16[40,3584]{1,0:T(8,128)(2,1)}, bf16[40,3584]{1,0:T(8,128)(2,1)}, bf16[40,3584]{1,0:T(8,128)(2,1)}, bf16[40,35...) fusion(bf16[1280,3584]{1,0:T(8,128)(2,1)} %scatter_custom_fusion), kind=kLoop, calls=%fused_computation.67 | loop fusion | bytes 10895360 | tf_op jit(solution)/shard_map/split | solution.py:76
  40.8 1.1 stack.99
  42.7 1.9 stack.100
  44.5 1.8 stack.101
  46.4 0.9 stack.102
  47.3 0.9 stack.103
  48.2 0.9 stack.104
  49.1 0.9 stack.105
  50.0 0.9 stack.106
  50.9 0.9 stack.107
  51.8 0.9 stack.108
  52.7 0.9 stack.109
  53.6 0.9 stack.110
  54.5 0.9 stack.111
  55.4 1.8 stack.112
  57.2 1.9 stack.113
  59.1 1.8 stack.114
  60.9 1.9 stack.115
  62.8 1.8 stack.116
  64.6 1.8 stack.117
  66.4 1.8 stack.118
  68.3 1.9 stack.119
  70.1 1.9 stack.120
  72.0 1.9 stack.121
  73.9 1.9 stack.122
  75.7 1.9 stack.123
  77.6 1.1 stack.124
  78.7 1.1 stack.125
  79.7 1.1 stack.126
  80.8 1.1 stack.127
  82.0 1.1 stack.129
  83.3 2.0 constant_dynamic-update-slice_fusion.30
  85.3 1.8 constant_dynamic-update-slice_fusion.29
  87.2 1.8 constant_dynamic-update-slice_fusion.28
  89.0 1.9 constant_dynamic-update-slice_fusion.27
  90.8 1.8 constant_dynamic-update-slice_fusion.26
  92.7 1.8 constant_dynamic-update-slice_fusion.25
  94.5 1.8 constant_dynamic-update-slice_fusion.24
  96.3 1.8 constant_dynamic-update-slice_fusion.23
  98.1 1.8 constant_dynamic-update-slice_fusion.22
  99.9 1.8 constant_dynamic-update-slice_fusion.21
  101.7 1.8 constant_dynamic-update-slice_fusion.20
  103.6 1.8 constant_dynamic-update-slice_fusion.19
  105.4 1.8 constant_dynamic-update-slice_fusion.18
  107.2 1.8 constant_dynamic-update-slice_fusion.17
  109.1 1.8 constant_dynamic-update-slice_fusion.16
  110.9 1.8 constant_dynamic-update-slice_fusion.15
  113.5 0.9 constant_dynamic-update-slice_fusion.13
  114.4 0.9 constant_dynamic-update-slice_fusion.12
  125.0 11.4 %copy.32 = bf16[32,8,5,3584]{3,1,2,0:T(8,128)(2,1)} copy(bf16[32,8,5,3584]{3,2,1,0:T(8,128)(2,1)} %constant_dynamic-update-slice_fusion) | data formatting | bytes 18350080 | tf_op jit(solution)/shard_map/stack | solution.py:76
  136.4 12.1 %all-to-all-start = ((bf16[32,8,5,3584]{3,1,2,0:T(8,128)(2,1)}), bf16[32,8,5,3584]{3,1,2,0:T(8,128)(2,1)}, u32[]{:S(2)}, u32[]{:S(2)}) async-start(bf16[32,8,5,3584]{3,1,2,0:T(8,128)(2,1)} %copy.32), calls=%async_computation | async-start | bytes 18350080 | tf_op jit(solution)/shard_map/all_to_all | solution.py:75
  150.5 35.2 %all-gather.3.cloned.1.call-done = bf16[3584,512]{1,0:T(8,128)(2,1)} async-done(((bf16[448,512]{1,0:T(8,128)(2,1)}), bf16[3584,512]{1,0:T(8,128)(2,1)}) %all-gather.3.cloned.1.call-update) | async-done | bytes 3670032 | tf_op jit(solution)/shard_map/all_gather | solution.py:80
  185.7 5.9 %copy.33 = bf16[3584,512]{0,1:T(8,128)(2,1)} copy(bf16[3584,512]{1,0:T(8,128)(2,1)} %all-gather.3.cloned.1.call-done) | data formatting | bytes 7340032 | tf_op jit(solution)/shard_map/all_gather | solution.py:80
  191.6 162.1 %all-to-all-done = bf16[32,8,5,3584]{3,1,2,0:T(8,128)(2,1)} async-done(((bf16[32,8,5,3584]{3,1,2,0:T(8,128)(2,1)}), bf16[32,8,5,3584]{3,1,2,0:T(8,128)(2,1)}, u32[]{:S(2)}, u32[]{:S(2)}) %all-to-all-start) | async-done | bytes 9175072 | tf_op jit(solution)/shard_map/all_to_all | solution.py:75
  353.8 12.3 %fusion.18 = f32[8,64,2048]{2,1,0:T(8,128)} fusion(bf16[8,160,2048]{2,1,0:T(8,128)(2,1)} %param.17, bf16[3584,8,64]{0,2,1:T(8,128)(2,1)} %bitcast.32, bf16[8,160,3584]{2,0,1:T(8,128)(2,1)} %bitcast.7), kind=kOutput, calls=%fused_computation.19 | convolution fusion | flops 922828800 | bytes 22282240 | tf_op jit(solution)/shard_map/esf,esr->fer/dot_general | solution.py:98
  366.1 5.3 %copy.35 = f32[2048,512]{1,0:T(8,128)} copy(f32[2048,512]{0,1:T(8,128)} %bitcast.31) | data formatting | bytes 8388608 | tf_op jit(solution)/shard_map/reshape | solution.py:100
  371.5 16.2 %fusion.1 = f32[8,64,3584]{2,1,0:T(8,128)} fusion(bf16[8,160,3584]{2,0,1:T(8,128)(2,1)} %bitcast.7, bf16[8,160,2048]{2,1,0:T(8,128)(2,1)} %param.17, bf16[2048,8,64]{0,2,1:T(8,128)(2,1)} %bitcast.33), kind=kOutput, calls=%fused_computation.3 | convolution fusion | flops 922828800 | bytes 23855104 | tf_op jit(solution)/shard_map/esd,esr->der/dot_general | solution.py:88
  387.7 8.4 %copy.38 = f32[3584,512]{1,0:T(8,128)} copy(f32[3584,512]{0,1:T(8,128)} %bitcast.30) | data formatting | bytes 14680064 | tf_op jit(solution)/shard_map/reshape | solution.py:90
  396.1 24.3 %reduce-scatter.3.cloned.1.call-done = f32[256,512]{1,0:T(8,128)} async-done(((f32[2048,512]{1,0:T(8,128)}), f32[256,512]{1,0:T(8,128)}) %reduce-scatter.3.cloned.1.call-update) | async-done | bytes 524304 | tf_op jit(solution)/shard_map/reduce_scatter | solution.py:99
  420.5 54.2 %reduce-scatter.5.cloned.1.call-done = f32[448,512]{1,0:T(8,128)} async-done(((f32[3584,512]{1,0:T(8,128)}), f32[448,512]{1,0:T(8,128)}) %reduce-scatter.5.cloned.1.call-update) | async-done | bytes 917520 | tf_op jit(solution)/shard_map/reduce_scatter | solution.py:89
  (69 shorter events, 19.5 us)
Async XLA Ops:
  42.7 39.2 %copy-start.9 = (bf16[40,3584]{1,0:T(8,128)(2,1)S(1)}, bf16[40,3584]{1,0:T(8,128)(2,1)}, u32[]{:S(2)}) copy-start(bf16[40,3584]{1,0:T(8,128)(2,1)} %get-tuple-element.4) | copy-start | bytes 860164
  47.3 35.8 %copy-start.8 = (bf16[40,3584]{1,0:T(8,128)(2,1)S(1)}, bf16[40,3584]{1,0:T(8,128)(2,1)}, u32[]{:S(2)}) copy-start(bf16[40,3584]{1,0:T(8,128)(2,1)} %get-tuple-element.2) | copy-start | bytes 860164
  83.3 29.4 %copy-start.7 = (bf16[1,8,5,3584]{3,2,1,0:T(8,128)(2,1)S(1)}, bf16[1,8,5,3584]{3,2,1,0:T(8,128)(2,1)}, u32[]{:S(2)}) copy-start(bf16[1,8,5,3584]{3,2,1,0:T(8,128)(2,1)} %stack.116) | copy-start | bytes 860164
  83.3 30.2 %copy-start.6 = (bf16[1,8,5,3584]{3,2,1,0:T(8,128)(2,1)S(1)}, bf16[1,8,5,3584]{3,2,1,0:T(8,128)(2,1)}, u32[]{:S(2)}) copy-start(bf16[1,8,5,3584]{3,2,1,0:T(8,128)(2,1)} %stack.117) | copy-start | bytes 860164
  83.3 31.1 %copy-start.5 = (bf16[1,8,5,3584]{3,2,1,0:T(8,128)(2,1)S(1)}, bf16[1,8,5,3584]{3,2,1,0:T(8,128)(2,1)}, u32[]{:S(2)}) copy-start(bf16[1,8,5,3584]{3,2,1,0:T(8,128)(2,1)} %stack.118) | copy-start | bytes 860164
  83.3 32.0 %copy-start.4 = (bf16[1,8,5,3584]{3,2,1,0:T(8,128)(2,1)S(1)}, bf16[1,8,5,3584]{3,2,1,0:T(8,128)(2,1)}, u32[]{:S(2)}) copy-start(bf16[1,8,5,3584]{3,2,1,0:T(8,128)(2,1)} %stack.119) | copy-start | bytes 860164
  83.3 32.8 %copy-start.3 = (bf16[1,8,5,3584]{3,2,1,0:T(8,128)(2,1)S(1)}, bf16[1,8,5,3584]{3,2,1,0:T(8,128)(2,1)}, u32[]{:S(2)}) copy-start(bf16[1,8,5,3584]{3,2,1,0:T(8,128)(2,1)} %stack.120) | copy-start | bytes 860164
  83.3 33.6 %copy-start.2 = (bf16[1,8,5,3584]{3,2,1,0:T(8,128)(2,1)S(1)}, bf16[1,8,5,3584]{3,2,1,0:T(8,128)(2,1)}, u32[]{:S(2)}) copy-start(bf16[1,8,5,3584]{3,2,1,0:T(8,128)(2,1)} %stack.121) | copy-start | bytes 860164
  83.3 34.4 %copy-start.1 = (bf16[1,8,5,3584]{3,2,1,0:T(8,128)(2,1)S(1)}, bf16[1,8,5,3584]{3,2,1,0:T(8,128)(2,1)}, u32[]{:S(2)}) copy-start(bf16[1,8,5,3584]{3,2,1,0:T(8,128)(2,1)} %stack.122) | copy-start | bytes 860164
  83.3 35.2 %copy-start = (bf16[1,8,5,3584]{3,2,1,0:T(8,128)(2,1)S(1)}, bf16[1,8,5,3584]{3,2,1,0:T(8,128)(2,1)}, u32[]{:S(2)}) copy-start(bf16[1,8,5,3584]{3,2,1,0:T(8,128)(2,1)} %stack.123) | copy-start | bytes 860164
  136.4 12.9 %copy-start.10 = (bf16[256,512]{1,0:T(8,128)(2,1)S(1)}, bf16[256,512]{1,0:T(8,128)(2,1)}, u32[]{:S(2)}) copy-start(bf16[256,512]{1,0:T(8,128)(2,1)} %param.18) | copy-start | bytes 786436
  136.4 217.3 %all-to-all-start = ((bf16[32,8,5,3584]{3,1,2,0:T(8,128)(2,1)}), bf16[32,8,5,3584]{3,1,2,0:T(8,128)(2,1)}, u32[]{:S(2)}, u32[]{:S(2)}) async-start(bf16[32,8,5,3584]{3,1,2,0:T(8,128)(2,1)} %copy.32), calls=%async_computation | async-start | bytes 18350080 | tf_op jit(solution)/shard_map/all_to_all | solution.py:75
  148.5 37.2 %all-gather.3.cloned.1.call-start = ((), (), s32[]{:S(2)}) async-start(), calls=%async_computation.3 | async-start | bytes 4128768 | tf_op jit(solution)/shard_map/all_gather | solution.py:80
  149.3 222.2 %all-gather.5.cloned.1.call-start = ((), (), s32[]{:S(2)}) async-start(), calls=%async_computation.5 | async-start | bytes 2359296 | tf_op jit(solution)/shard_map/all_gather | solution.py:67
  150.2 270.3 %reduce-scatter.3.cloned.1.call-start = ((), (), s32[]{:S(2)}) async-start(), calls=%async_computation.4 | async-start | bytes 4718592 | tf_op jit(solution)/shard_map/reduce_scatter | solution.py:99
  371.4 103.2 %reduce-scatter.5.cloned.1.call-start = ((), (), s32[]{:S(2)}) async-start(), calls=%async_computation.6 | async-start | bytes 8257536 | tf_op jit(solution)/shard_map/reduce_scatter | solution.py:89
Sparse Core Ops, SparseCore 0:
  151.2 34.4 all-gather.2
  188.1 29.2 all-gather.4
  371.6 48.8 reduce-scatter.2
  423.5 51.1 reduce-scatter.4
